TPU v7x, 32 devices: a whole 2x2x4 slice. The times are simulated.
32 devices in a mesh: seq: 8 (over z, y), head: 4 (over x, core).
Axes of the slice: x: 2, y: 2, z: 4, core: 2. Of those that a mesh axis runs over, the one named last changes fastest.
Arguments:
- block_in: bfloat16 [1, 2048, 1024], P(None, 'seq'), may hold values from -6 to 6
- upstream: bfloat16 [1, 2048, 1024], P(None, 'seq'), may hold values from -6 to 6
- first_gain: float32 [1024], replicated, may hold values from 0.5 to 1.5
- project_in: bfloat16 [1024, 4, 512], P(None, 'head'), may hold values from -0.1875 to 0.1875
- filter_taps: float32 [4, 4, 512], P(None, 'head'), may hold values from -2 to 2
- squeeze: bfloat16 [1024, 16], replicated, may hold values from -0.1875 to 0.1875
- expand: bfloat16 [16, 512], P(None, 'head'), may hold values from -0.75 to 0.75
- decay_bias: float32 [512], P('head'), may hold values from 0 to 16
- gating: bfloat16 [1024, 1024], P(None, 'head'), may hold values from -0.1875 to 0.1875
- head_scale: float32 [256], replicated, may hold values from 0.5 to 1.5
- project_out: bfloat16 [1024, 1024], P('head'), may hold values from -0.375 to 0.375
- second_gain: float32 [1024], replicated, may hold values from 0.5 to 1.5
- hidden_gate: bfloat16 [1024, 2816], P(None, 'head'), may hold values from -0.1875 to 0.1875
- hidden_lift: bfloat16 [1024, 2816], P(None, 'head'), may hold values from -0.1875 to 0.1875
- hidden_drop: bfloat16 [2816, 1024], P('head'), may hold values from -0.15625 to 0.15625
Outputs:
- block_out: bfloat16 [1, 2048, 1024], P(None, 'seq')
- input_grad: float32 [1, 2048, 1024], P(None, 'seq')
- grad_first: float32 [1024], replicated
- grad_project: float32 [1024, 4, 512], P('seq', 'head')
- grad_taps: float32 [4, 4, 512], P(None, 'head')
- grad_squeeze: float32 [1024, 16], replicated
- grad_expand: float32 [16, 512], P(None, 'head')
- grad_bias: float32 [512], P('head')
- grad_gating: float32 [1024, 1024], P('seq', 'head')
- grad_scale: float32 [256], replicated
- grad_output: float32 [1024, 1024], P('head', 'seq')
- grad_second: float32 [1024], replicated
- grad_gate: float32 [1024, 2816], P('seq', 'head')
- grad_lift: float32 [1024, 2816], P('seq', 'head')
- grad_drop: float32 [2816, 1024], P('head', 'seq')
All inputs are finite; a program needn't handle non-finite values.
Results may differ from a plain program's by a relative error of at most 0.02.
Values sent between devices are 32-bit elements; how exact they have to be, the bound alone decides.
A program may use at most 128 MiB of HBM per device.

v0:
```python
import jax
import jax.numpy as jnp
from jax import lax
from jax.sharding import PartitionSpec as P

GROUP = 64
EPS = 1e-05
NORMALIZER = 16.0
HIGH = lax.Precision.HIGHEST


def shifted(x, axis, by):
    size = lax.axis_size(axis)
    pairs = [(i, i + by) for i in range(size) if 0 <= i + by < size]
    return lax.ppermute(x, axis, pairs)


def entering(value, axis, join, neutral, backward):
    count, mine = (lax.axis_size(axis), lax.axis_index(axis))
    pieces = jax.tree.map(lambda part: lax.all_gather(part, axis), value)
    if backward:
        pieces = jax.tree.map(lambda part: part[::-1], pieces)
        mine = count - 1 - mine
    total = jax.tree.map(
        lambda part, zero: jnp.full_like(part, 0) + jnp.asarray(zero, part.dtype), value, neutral
    )

    def lap(position, total):
        longer = join(total, jax.tree.map(lambda part: part[position], pieces))
        return jax.tree.map(lambda new, old: jnp.where(position < mine, new, old), longer, total)

    return lax.fori_loop(0, count - 1, lap, total)


def product(left, right):
    return jnp.dot(left, right, preferred_element_type=jnp.float32)


def against(left, right):
    return lax.dot_general(
        left, right, (((1,), (1,)), ((), ())), preferred_element_type=jnp.float32
    )


def across(left, right):
    return lax.dot_general(
        left, right, (((0,), (0,)), ((), ())), preferred_element_type=jnp.float32
    )


def rms_scale(values):
    return lax.rsqrt(jnp.mean(values * values, axis=-1, keepdims=True) + EPS)


def rms_back(values, scale, gain, incoming):
    weighted = gain * incoming
    cube = scale * scale * scale
    return scale * weighted - values * cube * jnp.mean(values * weighted, axis=-1, keepdims=True)


def silu_grad(values):
    logistic = jax.nn.sigmoid(values)
    return logistic * (1.0 + values * (1.0 - logistic))


def causal_mask(size):
    rows = lax.broadcasted_iota(jnp.int32, (size, size), 0)
    columns = lax.broadcasted_iota(jnp.int32, (size, size), 1)
    return (columns <= rows).astype(jnp.float32)


def chain(earlier, later):
    return (earlier[0] * later[0], later[0][..., None] * earlier[1] + later[1])


def grouped(array, seqs, count):
    return array.reshape((seqs, count, GROUP) + array.shape[2:])


def local_states(decays, updates, backward):

    def step(carry, item):
        decay, update = item
        return (jnp.exp(decay)[..., None] * carry + update, carry)

    init = jnp.zeros_like(updates[:, 0])
    total, states = lax.scan(
        step, init, (jnp.moveaxis(decays, 1, 0), jnp.moveaxis(updates, 1, 0)), reverse=backward
    )
    return (jnp.moveaxis(states, 0, 1), total)


def body(
    block_in,
    upstream,
    first_gain,
    project_in,
    filter_taps,
    squeeze,
    expand,
    decay_bias,
    gating,
    head_scale,
    project_out,
    second_gain,
    hidden_gate,
    hidden_lift,
    hidden_drop,
):
    seqs, tokens, width = block_in.shape
    total_rows = seqs * tokens
    key_dim = expand.shape[1]
    value_dim = gating.shape[1]
    mixed_dim = project_in.shape[2]
    lags = filter_taps.shape[0] - 1
    count = tokens // GROUP
    taps = filter_taps.reshape(lags + 1, mixed_dim)
    weight_in = project_in.reshape(width, mixed_dim)
    residual_in = block_in.reshape(total_rows, width).astype(jnp.float32)
    scale_one = rms_scale(residual_in)
    normed_one = (residual_in * scale_one * first_gain).astype(jnp.bfloat16)
    projected = product(normed_one, weight_in).reshape(seqs, tokens, mixed_dim)
    before = shifted(projected[:, tokens - lags :], "seq", 1)
    padded = jnp.concatenate([before, projected], axis=1)
    filtered = taps[0] * projected
    for lag in range(1, lags + 1):
        filtered = filtered + taps[lag] * padded[:, lags - lag : lags - lag + tokens]
    activated_low = jax.nn.silu(filtered).astype(jnp.bfloat16)
    activated = lax.optimization_barrier(activated_low).astype(jnp.float32)
    root = key_dim ** (-0.5)
    query = grouped(activated[..., :key_dim] * root, seqs, count)
    keys = grouped(activated[..., key_dim : 2 * key_dim], seqs, count)
    values = grouped(activated[..., 2 * key_dim :], seqs, count)
    squeezed = product(normed_one, squeeze).astype(jnp.bfloat16)
    logits = product(squeezed, expand) + decay_bias
    log_decay = grouped(
        (jax.nn.log_sigmoid(logits) / NORMALIZER).reshape(seqs, tokens, key_dim), seqs, count
    )
    gate_in = product(normed_one, gating)
    mask = causal_mask(GROUP)
    running = jnp.einsum("ij,snjc->snic", mask, log_decay, precision=HIGH)
    last = running[:, :, -1]
    query_in = query * jnp.exp(running)
    key_in = keys * jnp.exp(-running)
    key_end = keys * jnp.exp(last[:, :, None] - running)
    scores = jnp.einsum("snic,snjc->snij", query_in, key_in, precision=HIGH) * mask
    updates = jnp.einsum("snjc,snjd->sncd", key_end, values, precision=HIGH)
    starts_zero, state_total = local_states(last, updates, False)
    decay_sum = jnp.sum(last, axis=1)
    decay_total = jnp.exp(decay_sum)
    identity = (jnp.ones_like(decay_total), jnp.zeros_like(state_total))
    incoming = entering((decay_total, state_total), "seq", chain, identity, False)[1]
    before_group = jnp.cumsum(last, axis=1) - last
    starts = starts_zero + jnp.exp(before_group)[..., None] * incoming[:, None]
    mixed = jnp.einsum("snij,snjd->snid", scores, values, precision=HIGH)
    mixed = mixed + jnp.einsum("snic,sncd->snid", query_in, starts, precision=HIGH)
    mixed = mixed.reshape(total_rows, value_dim)
    scale_head = rms_scale(mixed)
    normed_head = mixed * scale_head * head_scale
    gated = (normed_head * jax.nn.silu(gate_in)).astype(jnp.bfloat16)
    branch = lax.psum(product(gated, project_out), "head")
    residual = residual_in + branch
    scale_two = rms_scale(residual)
    normed_two = (residual * scale_two * second_gain).astype(jnp.bfloat16)
    gate_value = product(normed_two, hidden_gate)
    lift_value = product(normed_two, hidden_lift)
    inner = (jax.nn.silu(gate_value) * lift_value).astype(jnp.bfloat16)
    feed = lax.psum(product(inner, hidden_drop), "head")
    block_out = (residual + feed).astype(jnp.bfloat16).reshape(seqs, tokens, width)
    seed = upstream.reshape(total_rows, width)
    grad_drop = across(inner, seed)
    grad_inner = against(seed, hidden_drop)
    grad_gv = (grad_inner * lift_value * silu_grad(gate_value)).astype(jnp.bfloat16)
    grad_lv = (grad_inner * jax.nn.silu(gate_value)).astype(jnp.bfloat16)
    grad_gate = across(normed_two, grad_gv)
    grad_lift = across(normed_two, grad_lv)
    feed_grads = (
        lax.psum_scatter(grad_gate, "seq", scatter_dimension=0, tiled=True),
        lax.psum_scatter(grad_lift, "seq", scatter_dimension=0, tiled=True),
        lax.psum_scatter(grad_drop, "seq", scatter_dimension=1, tiled=True),
    )
    grad_two = lax.psum(against(grad_gv, hidden_gate) + against(grad_lv, hidden_lift), "head")
    grad_second = jnp.sum(grad_two * residual * scale_two, axis=0)
    grad_resid = seed.astype(jnp.float32) + rms_back(residual, scale_two, second_gain, grad_two)
    resid_low = grad_resid.astype(jnp.bfloat16)
    grad_output = across(gated, resid_low)
    grad_gated = against(resid_low, project_out)
    grad_gatein = (grad_gated * normed_head * silu_grad(gate_in)).astype(jnp.bfloat16)
    grad_normhead = grad_gated * jax.nn.silu(gate_in)
    grad_scale = jnp.sum(grad_normhead * mixed * scale_head, axis=0)
    grad_mixed_low = rms_back(mixed, scale_head, head_scale, grad_normhead).astype(jnp.bfloat16)
    grad_mixed = lax.optimization_barrier(grad_mixed_low).astype(jnp.float32)
    outgrad = grouped(grad_mixed.reshape(seqs, tokens, value_dim), seqs, count)
    query_end = jnp.einsum("snic,snid->sncd", query_in, outgrad, precision=HIGH)
    following_zero, back_total = local_states(last, query_end, True)
    after = entering((decay_total, back_total), "seq", chain, identity, True)[1]
    after_group = decay_sum[:, None] - jnp.cumsum(last, axis=1)
    following = following_zero + jnp.exp(after_group)[..., None] * after[:, None]
    inner_group = jnp.einsum("snid,snjd->snij", outgrad, values, precision=HIGH) * mask
    grad_query = jnp.exp(running) * (
        jnp.einsum("snij,snjc->snic", inner_group, key_in, precision=HIGH)
        + jnp.einsum("snid,sncd->snic", outgrad, starts, precision=HIGH)
    )
    grad_keys = jnp.exp(-running) * jnp.einsum(
        "snij,snic->snjc", inner_group, query_in, precision=HIGH
    )
    grad_keys = grad_keys + jnp.exp(last[:, :, None] - running) * jnp.einsum(
        "snjd,sncd->snjc", values, following, precision=HIGH
    )
    grad_values = jnp.einsum("snij,snid->snjd", scores, outgrad, precision=HIGH)
    grad_values = grad_values + jnp.einsum("snjc,sncd->snjd", key_end, following, precision=HIGH)
    grad_running = (query * grad_query - keys * grad_keys).reshape(seqs, tokens, key_dim)
    state_end = decay_total[..., None] * incoming + state_total
    beyond = jnp.sum(state_end * after, axis=-1)
    upper = jnp.transpose(causal_mask(tokens))
    suffix = jnp.einsum("ij,sjc->sic", upper, grad_running, precision=HIGH)
    grad_log = suffix + beyond[:, None]
    grad_act = jnp.concatenate(
        [
            grad_query.reshape(seqs, tokens, key_dim) * root,
            grad_keys.reshape(seqs, tokens, key_dim),
            grad_values.reshape(seqs, tokens, value_dim),
        ],
        axis=-1,
    )
    grad_filtered = grad_act * silu_grad(filtered)
    later = shifted(grad_filtered[:, :lags], "seq", -1)
    padded_back = jnp.concatenate([grad_filtered, later], axis=1)
    grad_projected = taps[0] * grad_filtered
    tap_rows = [jnp.sum(grad_filtered * projected, axis=(0, 1))]
    for lag in range(1, lags + 1):
        grad_projected = grad_projected + taps[lag] * padded_back[:, lag : lag + tokens]
        tap_rows.append(
            jnp.sum(grad_filtered * padded[:, lags - lag : lags - lag + tokens], axis=(0, 1))
        )
    grad_taps = jnp.stack(tap_rows).reshape(lags + 1, 1, mixed_dim)
    grad_projected = grad_projected.reshape(total_rows, mixed_dim).astype(jnp.bfloat16)
    grad_logits = grad_log.reshape(total_rows, key_dim) * jax.nn.sigmoid(-logits) / NORMALIZER
    grad_bias = jnp.sum(grad_logits, axis=0)
    logits_low = grad_logits.astype(jnp.bfloat16)
    grad_expand = across(squeezed, logits_low)
    squeeze_low = against(logits_low, expand).astype(jnp.bfloat16)
    grad_squeeze = across(normed_one, squeeze_low)
    grad_project = across(normed_one, grad_projected).reshape(width, 1, mixed_dim)
    grad_gating = across(normed_one, grad_gatein)
    partial_value = (
        against(grad_projected, weight_in)
        + against(grad_gatein, gating)
        + against(squeeze_low, squeeze)
    )
    grad_one = lax.psum(partial_value, "head")
    grad_first = jnp.sum(grad_one * residual_in * scale_one, axis=0)
    input_grad = (grad_resid + rms_back(residual_in, scale_one, first_gain, grad_one)).reshape(
        seqs, tokens, width
    )
    mixer_grads = (
        lax.psum_scatter(grad_project, "seq", scatter_dimension=0, tiled=True),
        lax.psum_scatter(grad_gating, "seq", scatter_dimension=0, tiled=True),
        lax.psum_scatter(grad_output, "seq", scatter_dimension=1, tiled=True),
    )
    summed = tuple(mixer_grads) + tuple(feed_grads)
    small_head = lax.psum((grad_taps, grad_expand, grad_bias, grad_first, grad_second), "seq")
    shared = lax.psum((grad_scale, grad_squeeze), ("seq", "head"))
    return (
        block_out,
        input_grad,
        small_head[3],
        summed[0],
        small_head[0],
        shared[1],
        small_head[1],
        small_head[2],
        summed[1],
        shared[0],
        summed[2],
        small_head[4],
        summed[3],
        summed[4],
        summed[5],
    )


def solution(mesh):
    in_specs = (
        P(None, "seq", None),
        P(None, "seq", None),
        P(),
        P(None, "head", None),
        P(None, "head", None),
        P(),
        P(None, "head"),
        P("head"),
        P(None, "head"),
        P(),
        P("head", None),
        P(),
        P(None, "head"),
        P(None, "head"),
        P("head", None),
    )
    out_specs = (
        P(None, "seq", None),
        P(None, "seq", None),
        P(),
        P("seq", "head", None),
        P(None, "head", None),
        P(),
        P(None, "head"),
        P("head"),
        P("seq", "head"),
        P(),
        P("head", "seq"),
        P(),
        P("seq", "head"),
        P("seq", "head"),
        P("head", "seq"),
    )
    return jax.shard_map(body, mesh=mesh, in_specs=in_specs, out_specs=out_specs, check_vma=False)
```

profile of v0, /device:TPU:0, one launch (start us, length us, event | category | flops | bytes accessed | tf_op | source)
XLA Modules:
  0.0 871.2 jit_solution(14256679517528602044)
XLA Ops:
  11.2 4.9 collective-permute-start
  20.4 4.3 while.58
  26.0 21.5 %all-gather.3 = f32[8,1,128]{2,1,0:T(1,128)S(1)} all-gather(f32[1,1,128]{2,1,0:T(1,128)S(1)} %get-tuple-element.555), channel_id=2, replica_groups=mesh['seq'=8,'head'=4] {'seq'}, dimensions={0}, use_global_device_ids=true | all-gather | bytes 4608 | tf_op jit(solution)/shard_map/all_gather | solution.py:20
  49.4 18.3 %all-gather.7.cloned.1.call-done = f32[8,128,256]{2,1,0:T(8,128)} async-done(((f32[1,128,256]{2,1,0:T(8,128)}), f32[8,128,256]{2,1,0:T(8,128)}) %all-gather.7.cloned.1.call-update) | async-done | bytes 1048592 | tf_op jit(solution)/shard_map/all_gather | solution.py:20
  67.7 7.3 while.59
  80.8 35.1 %all-reduce.7.cloned.1.call-done = f32[256,1024]{1,0:T(8,128)} async-done(((f32[256,1024]{1,0:T(8,128)}), f32[256,1024]{1,0:T(8,128)}) %all-reduce.7.cloned.1.call-update) | async-done | bytes 1048592 | tf_op jit(solution)/shard_map/psum | solution.py:161
  126.5 35.6 %all-reduce.9.cloned.1.call-done = f32[256,1024]{1,0:T(8,128)} async-done(((f32[256,1024]{1,0:T(8,128)}), f32[256,1024]{1,0:T(8,128)}) %all-reduce.9.cloned.1.call-update) | async-done | bytes 1048592 | tf_op jit(solution)/shard_map/psum | solution.py:182
  170.1 9.2 %while.60 = (s32[]{:T(128)}, f32[1,128,256]{2,1,0:T(8,128)S(1)}, f32[4,1,128,256]{3,2,1,0:T(8,128)}, f32[4,1,128]{2,1,0:T(1,128)}, f32[4,1,128,256]{3,2,1,0:T(8,128)}, /*index=5*/s32[]{:T(128)}, s32[]{:T(128)}, s32[]{:T(128)}) while((s32[]{:T(128)}, f32[1,128,256]{2,1,0:T(8,128)S(1)}, f32[4,1,128,256]{3,2,1,0:T(8,128)}, ...), condition=%wide.region_15.16_spmd.clone, body=%wide.region_14.15_spmd.clone.sunk | while | flops 131076 | bytes 657016 | solution.py:87
  180.9 2.6 fusion.121
  187.3 33.6 %all-gather.9.cloned.1.call-done = f32[8,128,256]{2,1,0:T(8,128)} async-done(((f32[1,128,256]{2,1,0:T(8,128)}), f32[8,128,256]{2,1,0:T(8,128)}) %all-gather.9.cloned.1.call-update) | async-done | bytes 1048592 | tf_op jit(solution)/shard_map/all_gather | solution.py:20
  223.2 15.3 %while.61 = (s32[]{:T(128)}, f32[1,128,256]{2,1,0:T(8,128)S(1)}, s32[]{:T(128)}, f32[8,1,128]{2,1,0:T(1,128)}, f32[8,1,128,256]{3,2,1,0:T(8,128)}, /*index=5*/s32[]{:T(128)}, s32[]{:T(128)}) while((s32[]{:T(128)}, f32[1,128,256]{2,1,0:T(8,128)S(1)}, s32[]{:T(128)}, f32[8,1,128]{2,1,0:T(1,128)}, f32[8,1,128,256]{3,2,1,0:T(8,128)}, ...), condition=%wide.region_17.18_spmd.clone, body=%wide.region_16.17_spmd.clone.sunk | while | flops 131076 | bytes 394857 | solution.py:32
  259.6 3.1 fusion.124
  262.8 3.2 fusion.125
  267.0 3.2 fusion.51
  270.8 38.8 %psum.86 = f32[256]{0:T(256)} all-reduce(f32[256]{0:T(256)S(1)} %copy-done.89), channel_id=1, replica_groups=mesh['seq'=8,'head'=4] {'seq','head'}, use_global_device_ids=true, to_apply=%region_35.36 | all-reduce | flops 256 | bytes 2048 | tf_op jit(solution)/shard_map/psum | solution.py:263
  311.4 37.7 %all-reduce = (f32[1024]{0:T(1024)}, f32[4,1,512]{2,1,0:T(1,128)}, f32[16,128]{1,0:T(8,128)}, f32[128]{0:T(128)}, f32[1024]{0:T(1024)}) all-reduce(f32[1024]{0:T(1024)S(1)} %get-tuple-element.475, f32[4,1,512]{2,1,0:T(1,128)S(1)} %reshape.447, f32[16,128]{1,0:T(8,128)S(1)} %fusion.99, ...), channel_id=1, replica_groups=mesh['seq'=8,'head'=4] {'seq'}, use_global_device_ids=true, to_apply=%region_22.23 | all-reduce | flops 6272 | bytes 50176 | tf_op jit(solution)/shard_map/psum | solution.py:262
  349.1 3.4 fusion.27
  352.5 21.5 %reduce-scatter.7.cloned.1.call-done = f32[128,1,512]{2,0,1:T(8,128)} async-done(((f32[1024,1,512]{2,0,1:T(8,128)}), f32[128,1,512]{2,0,1:T(8,128)}) %reduce-scatter.7.cloned.1.call-update) | async-done | bytes 262160 | tf_op jit(solution)/shard_map/reduce_scatter | solution.py:257
  376.0 122.0 %all-reduce.11.cloned.1.call-done = f32[1024,16]{0,1:T(8,128)} async-done(((f32[1024,16]{0,1:T(8,128)}), f32[1024,16]{0,1:T(8,128)}) %all-reduce.11.cloned.1.call-update) | async-done | bytes 65552 | tf_op jit(solution)/shard_map/psum | solution.py:263
  498.0 69.9 %reduce-scatter.11.cloned.1.call-done = f32[256,128]{1,0:T(8,128)} async-done(((f32[256,1024]{1,0:T(8,128)}), f32[256,128]{1,0:T(8,128)}) %reduce-scatter.11.cloned.1.call-update) | async-done | bytes 131088 | tf_op jit(solution)/shard_map/reduce_scatter | solution.py:259
  567.9 67.2 %reduce-scatter.9.cloned.1.call-done = f32[128,256]{1,0:T(8,128)} async-done(((f32[1024,256]{1,0:T(8,128)}), f32[128,256]{1,0:T(8,128)}) %reduce-scatter.9.cloned.1.call-update) | async-done | bytes 131088 | tf_op jit(solution)/shard_map/reduce_scatter | solution.py:258
  635.2 75.6 %reduce-scatter.13.cloned.1.call-done = f32[128,704]{0,1:T(8,128)} async-done(((f32[1024,704]{0,1:T(8,128)}), f32[128,704]{0,1:T(8,128)}) %reduce-scatter.13.cloned.1.call-update) | async-done | bytes 360464 | tf_op jit(solution)/shard_map/reduce_scatter | solution.py:178
  710.8 76.2 %reduce-scatter.15.cloned.1.call-done = f32[128,704]{0,1:T(8,128)} async-done(((f32[1024,704]{0,1:T(8,128)}), f32[128,704]{0,1:T(8,128)}) %reduce-scatter.15.cloned.1.call-update) | async-done | bytes 360464 | tf_op jit(solution)/shard_map/reduce_scatter | solution.py:179
  787.0 75.9 %reduce-scatter.17.cloned.1.call-done = f32[704,128]{1,0:T(8,128)} async-done(((f32[704,1024]{1,0:T(8,128)}), f32[704,128]{1,0:T(8,128)}) %reduce-scatter.17.cloned.1.call-update) | async-done | bytes 360464 | tf_op jit(solution)/shard_map/reduce_scatter | solution.py:180
  (343 shorter events, 105.8 us)
Async XLA Ops:
  7.2 113.7 %copy-start = (bf16[704,1024]{1,0:T(8,128)(2,1)S(1)}, bf16[704,1024]{1,0:T(8,128)(2,1)}, u32[]{:S(2)}) copy-start(bf16[704,1024]{1,0:T(8,128)(2,1)} %param.37) | copy-start | bytes 4325380
  7.2 60.5 %all-gather.7.cloned.1.call-start = ((), (), s32[]{:S(2)}) async-start(), calls=%async_computation.15 | async-start | bytes 1179648 | tf_op jit(solution)/shard_map/all_gather | solution.py:20
  11.2 6.3 collective-permute-start
  18.7 49.0 %copy-start.12 = (f32[1,256,128]{2,1,0:T(8,128)}, f32[1,256,128]{2,1,0:T(8,128)S(1)}, u32[]{:S(2)}) copy-start(f32[1,256,128]{2,1,0:T(8,128)S(1)} %slice.81) | copy-start | bytes 393220
  19.1 148.3 %copy-start.24 = (f32[1,4,64,128]{3,2,1,0:T(8,128)}, f32[1,4,64,128]{3,2,1,0:T(8,128)S(1)}, u32[]{:S(2)}) copy-start(f32[1,4,64,128]{3,2,1,0:T(8,128)S(1)} %get-tuple-element.558) | copy-start | bytes 393220
  24.7 50.9 %copy-start.16 = (f32[4,1,128,256]{3,2,1,0:T(8,128)}, f32[4,1,128,256]{3,2,1,0:T(8,128)S(1)}, u32[]{:S(2)}) copy-start(f32[4,1,128,256]{3,2,1,0:T(8,128)S(1)} %get-tuple-element.335) | copy-start | bytes 1572868
  25.3 90.6 %all-reduce.7.cloned.1.call-start = ((), (), s32[]{:S(2)}) async-start(), calls=%async_computation.6 | async-start | bytes 2097152 | tf_op jit(solution)/shard_map/psum | solution.py:161
  25.4 42.3 %copy-start.47 = (f32[64,64]{1,0:T(8,128)}, f32[64,64]{1,0:T(8,128)S(1)}, u32[]{:S(2)}) copy-start(f32[64,64]{1,0:T(8,128)S(1)} %fusion.102) | copy-start | bytes 49156
  80.8 81.4 %all-reduce.9.cloned.1.call-start = ((), (), s32[]{:S(2)}) async-start(), calls=%async_computation.7 | async-start | bytes 2097152 | tf_op jit(solution)/shard_map/psum | solution.py:182
  125.2 95.7 %all-gather.9.cloned.1.call-start = ((), (), s32[]{:S(2)}) async-start(), calls=%async_computation.16 | async-start | bytes 1179648 | tf_op jit(solution)/shard_map/all_gather | solution.py:20
  180.0 129.8 %all-reduce.13.cloned.1.call-start = ((), (), s32[]{:S(2)}) async-start(), calls=%async_computation.17 | async-start | bytes 4194304 | tf_op jit(solution)/shard_map/psum | solution.py:168
  243.0 5.7 collective-permute-start.1
  251.5 122.5 %reduce-scatter.7.cloned.1.call-start = ((), (), s32[]{:S(2)}) async-start(), calls=%async_computation.8 | async-start | bytes 2359296 | tf_op jit(solution)/shard_map/reduce_scatter | solution.py:257
  253.5 244.6 %all-reduce.11.cloned.1.call-start = ((), (), s32[]{:S(2)}) async-start(), calls=%async_computation.9 | async-start | bytes 131072 | tf_op jit(solution)/shard_map/psum | solution.py:263
  254.5 313.5 %reduce-scatter.11.cloned.1.call-start = ((), (), s32[]{:S(2)}) async-start(), calls=%async_computation.11 | async-start | bytes 1179648 | tf_op jit(solution)/shard_map/reduce_scatter | solution.py:259
  257.1 378.0 %reduce-scatter.9.cloned.1.call-start = ((), (), s32[]{:S(2)}) async-start(), calls=%async_computation.10 | async-start | bytes 1179648 | tf_op jit(solution)/shard_map/reduce_scatter | solution.py:258
  259.6 451.2 %reduce-scatter.13.cloned.1.call-start = ((), (), s32[]{:S(2)}) async-start(), calls=%async_computation.12 | async-start | bytes 3244032 | tf_op jit(solution)/shard_map/reduce_scatter | solution.py:178
  262.7 524.2 %reduce-scatter.15.cloned.1.call-start = ((), (), s32[]{:S(2)}) async-start(), calls=%async_computation.13 | async-start | bytes 3244032 | tf_op jit(solution)/shard_map/reduce_scatter | solution.py:179
  266.0 596.9 %reduce-scatter.17.cloned.1.call-start = ((), (), s32[]{:S(2)}) async-start(), calls=%async_computation.14 | async-start | bytes 3244032 | tf_op jit(solution)/shard_map/reduce_scatter | solution.py:180
  270.2 39.5 %copy-start.51 = (bf16[256,128]{1,0:T(8,128)(2,1)S(1)}, bf16[256,128]{1,0:T(8,128)(2,1)}, u32[]{:S(2)}) copy-start(bf16[256,128]{1,0:T(8,128)(2,1)} %copy-done.50) | copy-start | bytes 196612
  270.2 39.5 %copy-start.80 = (bf16[256,16]{0,1:T(8,128)(2,1)S(1)}, bf16[256,16]{0,1:T(8,128)(2,1)}, u32[]{:S(2)}) copy-start(bf16[256,16]{0,1:T(8,128)(2,1)} %copy-done.79) | copy-start | bytes 24580
  270.2 41.2 %copy-start.71 = (f32[1024]{0:T(1024)S(1)}, f32[1024]{0:T(1024)}, u32[]{:S(2)}) copy-start(f32[1024]{0:T(1024)} %get-tuple-element.473) | copy-start | bytes 12292
  270.2 41.2 %copy-start.90 = (f32[128]{0:T(128)S(1)}, f32[128]{0:T(128)}, u32[]{:S(2)}) copy-start(f32[128]{0:T(128)} %get-tuple-element.566) | copy-start | bytes 1540
  270.2 78.9 %copy-start.85 = (f32[256]{0:T(256)S(1)}, f32[256]{0:T(256)}, u32[]{:S(2)}) copy-start(f32[256]{0:T(256)} %get-tuple-element.550) | copy-start | bytes 3076
  (83 other events, 491.2 us)
Sparse Core Ops, SparseCore 0:
  25.4 42.2 all-gather.6
  80.9 34.9 all-reduce.6
  125.4 36.7 all-reduce.8
  180.1 40.7 all-gather.8
  251.6 50.4 all-reduce.12
  305.5 68.4 reduce-scatter.6
  379.6 118.3 all-reduce.10
  502.0 65.8 reduce-scatter.10
  571.9 63.1 reduce-scatter.8
  639.1 71.6 reduce-scatter.12
  714.9 71.9 reduce-scatter.14
  791.0 71.8 reduce-scatter.16
where the time goes:
time: 873 us; the launch traced here: 871 us
  waiting for transfers between devices  634 us (73%)
  blocking collectives  98 us (11%)
  matrix products  47.6 us (5%)
  other arithmetic  42.4 us (5%)
  local copies, waits for them, and re-layouts  26.4 us (3%)
  between operations  15.4 us (2%)
    psum x1, waiting for transfers between devices, body(): shared = lax.psum((grad_scale, grad_squeeze), ('seq', 'head'))  122 us
    reduce_scatter x1, waiting for transfers between devices, body(): lax.psum_scatter(grad_lift, 'seq', scatter_dimension=0, tiled=True)  76.2 us
    reduce_scatter x1, waiting for transfers between devices, body(): lax.psum_scatter(grad_drop, 'seq', scatter_dimension=1, tiled=True)  75.9 us
    reduce_scatter x1, waiting for transfers between devices, body(): lax.psum_scatter(grad_gate, 'seq', scatter_dimension=0, tiled=True)  75.6 us
    reduce_scatter x1, waiting for transfers between devices, body(): lax.psum_scatter(grad_output, 'seq', scatter_dimension=1, tiled=True)  69.9 us
    reduce_scatter x1, waiting for transfers between devices, body(): lax.psum_scatter(grad_gating, 'seq', scatter_dimension=0, tiled=True)  67.2 us
    all_gather x2, waiting for transfers between devices, entering(): pieces = jax.tree.map(lambda part: lax.all_gather(part, axis), value)  51.9 us
    psum x1, blocking collectives, body(): shared = lax.psum((grad_scale, grad_squeeze), ('seq', 'head'))  38.8 us
  transfers between devices with their start and end apart: 14, of which 12 were waited for; matrix products, arithmetic and copies ran while one was open for 4% of the time, Pallas kernels for 0%

commit v1 on v0

--- a/solution.py
+++ b/solution.py
@@ -260,7 +260,8 @@
     )
     summed = tuple(mixer_grads) + tuple(feed_grads)
     small_head = lax.psum((grad_taps, grad_expand, grad_bias, grad_first, grad_second), "seq")
-    shared = lax.psum((grad_scale, grad_squeeze), ("seq", "head"))
+    half = lax.psum((grad_scale, grad_squeeze), "head")
+    shared = lax.psum(half, "seq")
     return (
         block_out,
         input_grad,

time: 873 us -> 822 us (0.942)
  blocking collectives: 98 us -> 65.3 us
  waiting for transfers between devices: 634 us -> 615 us
    psum x1, waiting for transfers between devices: 122 us -> 71.6 us  [body(): shared = lax.psum(half, 'seq')]
    psum x1, waiting for transfers between devices: 0.01 us -> 43.4 us  [body(): feed = lax.psum(product(inner, hidden_drop), 'head')]
    psum x1, blocking collectives: 38.8 us -> 6.03 us  [body(): half = lax.psum((grad_scale, grad_squeeze), 'head')]
    reduce_scatter x1, waiting for transfers between devices: 21.5 us -> 11.7 us  [body(): lax.psum_scatter(grad_project, 'seq', scatter_dimension=0, tiled=True)]
  transfers between devices with their start and end apart: 14 -> 14, of which waited for: 12 -> 13; matrix products, arithmetic and copies ran while one was open for 4% -> 4% of each run, Pallas kernels for 0% -> 0%
where the time goes in v1:
time: 822 us; the launch traced here: 820 us
  waiting for transfers between devices  615 us (75%)
  blocking collectives  65.3 us (8%)
  matrix products  47.5 us (6%)
  other arithmetic  42.4 us (5%)
  local copies, waits for them, and re-layouts  27.2 us (3%)
  between operations  15.3 us (2%)
    reduce_scatter x1, waiting for transfers between devices, body(): lax.psum_scatter(grad_gate, 'seq', scatter_dimension=0, tiled=True)  76.9 us
    reduce_scatter x1, waiting for transfers between devices, body(): lax.psum_scatter(grad_drop, 'seq', scatter_dimension=1, tiled=True)  76.2 us
    reduce_scatter x1, waiting for transfers between devices, body(): lax.psum_scatter(grad_lift, 'seq', scatter_dimension=0, tiled=True)  76.1 us
    psum x1, waiting for transfers between devices, body(): shared = lax.psum(half, 'seq')  71.6 us
    reduce_scatter x1, waiting for transfers between devices, body(): lax.psum_scatter(grad_gating, 'seq', scatter_dimension=0, tiled=True)  67.1 us
    reduce_scatter x1, waiting for transfers between devices, body(): lax.psum_scatter(grad_output, 'seq', scatter_dimension=1, tiled=True)  65.7 us
    all_gather x2, waiting for transfers between devices, entering(): pieces = jax.tree.map(lambda part: lax.all_gather(part, axis), value)  51.8 us
    psum x1, waiting for transfers between devices, body(): feed = lax.psum(product(inner, hidden_drop), 'head')  43.4 us
  transfers between devices with their start and end apart: 14, of which 13 were waited for; matrix products, arithmetic and copies ran while one was open for 4% of the time, Pallas kernels for 0%

profile of v1, /device:TPU:0, one launch (start us, length us, event | category | flops | bytes accessed | tf_op | source)
XLA Modules:
  0.0 820.2 jit_solution(11301531786532587570)
XLA Ops:
  11.1 4.9 collective-permute-start
  20.3 4.3 while.58
  25.9 21.5 %all-gather.3 = f32[8,1,128]{2,1,0:T(1,128)S(1)} all-gather(f32[1,1,128]{2,1,0:T(1,128)S(1)} %get-tuple-element.557), channel_id=2, replica_groups=mesh['seq'=8,'head'=4] {'seq'}, dimensions={0}, use_global_device_ids=true | all-gather | bytes 4608 | tf_op jit(solution)/shard_map/all_gather | solution.py:20
  49.4 18.3 %all-gather.7.cloned.1.call-done = f32[8,128,256]{2,1,0:T(8,128)} async-done(((f32[1,128,256]{2,1,0:T(8,128)}), f32[8,128,256]{2,1,0:T(8,128)}) %all-gather.7.cloned.1.call-update) | async-done | bytes 1048592 | tf_op jit(solution)/shard_map/all_gather | solution.py:20
  67.7 7.3 while.59
  80.8 35.1 %all-reduce.7.cloned.1.call-done = f32[256,1024]{1,0:T(8,128)} async-done(((f32[256,1024]{1,0:T(8,128)}), f32[256,1024]{1,0:T(8,128)}) %all-reduce.7.cloned.1.call-update) | async-done | bytes 1048592 | tf_op jit(solution)/shard_map/psum | solution.py:161
  126.4 35.7 %all-reduce.9.cloned.1.call-done = f32[256,1024]{1,0:T(8,128)} async-done(((f32[256,1024]{1,0:T(8,128)}), f32[256,1024]{1,0:T(8,128)}) %all-reduce.9.cloned.1.call-update) | async-done | bytes 1048592 | tf_op jit(solution)/shard_map/psum | solution.py:182
  170.0 9.4 %while.60 = (s32[]{:T(128)}, f32[1,128,256]{2,1,0:T(8,128)S(1)}, f32[4,1,128,256]{3,2,1,0:T(8,128)}, f32[4,1,128]{2,1,0:T(1,128)}, f32[4,1,128,256]{3,2,1,0:T(8,128)}, /*index=5*/s32[]{:T(128)}, s32[]{:T(128)}, s32[]{:T(128)}) while((s32[]{:T(128)}, f32[1,128,256]{2,1,0:T(8,128)S(1)}, f32[4,1,128,256]{3,2,1,0:T(8,128)}, ...), condition=%wide.region_15.16_spmd.clone, body=%wide.region_14.15_spmd.clone.sunk | while | flops 131076 | bytes 657016 | solution.py:87
  187.4 33.6 %all-gather.9.cloned.1.call-done = f32[8,128,256]{2,1,0:T(8,128)} async-done(((f32[1,128,256]{2,1,0:T(8,128)}), f32[8,128,256]{2,1,0:T(8,128)}) %all-gather.9.cloned.1.call-update) | async-done | bytes 1048592 | tf_op jit(solution)/shard_map/all_gather | solution.py:20
  223.3 15.3 %while.61 = (s32[]{:T(128)}, f32[1,128,256]{2,1,0:T(8,128)S(1)}, s32[]{:T(128)}, f32[8,1,128]{2,1,0:T(1,128)}, f32[8,1,128,256]{3,2,1,0:T(8,128)}, /*index=5*/s32[]{:T(128)}, s32[]{:T(128)}) while((s32[]{:T(128)}, f32[1,128,256]{2,1,0:T(8,128)S(1)}, s32[]{:T(128)}, f32[8,1,128]{2,1,0:T(1,128)}, f32[8,1,128,256]{3,2,1,0:T(8,128)}, ...), condition=%wide.region_17.18_spmd.clone, body=%wide.region_16.17_spmd.clone.sunk | while | flops 131076 | bytes 394857 | solution.py:32
  246.9 3.3 collective-permute-done.1
  261.0 43.4 %all-reduce.13.cloned.1.call-done = (f32[256,1024]{1,0:T(8,128)}, f32[256,1024]{1,0:T(8,128)}, f32[1024,16]{0,1:T(8,128)}) async-done(((f32[256,1024]{1,0:T(8,128)}, f32[256,1024]{1,0:T(8,128)}, f32[1024,16]{0,1:T(8,128)}), (f32[256,1024]{1,0:T(8,128)}, f32[256,1024]{1,0:T(8,128)}, f32[1024,16]{0,1:T(8,128)})) %all-reduce.13.cloned.1.call-update) | async-done | bytes 2162704 | tf_op jit(solution)/shard_map/psum | solution.py:168
  307.6 3.1 fusion.125
  311.8 3.2 fusion.51
  315.6 6.0 psum.101
  323.4 37.7 %all-reduce = (f32[1024]{0:T(1024)}, f32[4,1,512]{2,1,0:T(1,128)}, f32[16,128]{1,0:T(8,128)}, f32[128]{0:T(128)}, f32[256]{0:T(256)}, /*index=5*/f32[1024]{0:T(1024)}) all-reduce(f32[1024]{0:T(1024)S(1)} %get-tuple-element.475, f32[4,1,512]{2,1,0:T(1,128)S(1)} %reshape.447, ...), channel_id=1, replica_groups=mesh['seq'=8,'head'=4] {'seq'}, use_global_device_ids=true, to_apply=%region_22.23 | all-reduce | flops 6528 | bytes 52224 | tf_op jit(solution)/shard_map/psum | solution.py:262
  361.1 3.5 fusion.27
  364.6 11.7 %reduce-scatter.7.cloned.1.call-done = f32[128,1,512]{2,0,1:T(8,128)} async-done(((f32[1024,1,512]{2,0,1:T(8,128)}), f32[128,1,512]{2,0,1:T(8,128)}) %reduce-scatter.7.cloned.1.call-update) | async-done | bytes 262160 | tf_op jit(solution)/shard_map/reduce_scatter | solution.py:257
  378.3 65.7 %reduce-scatter.11.cloned.1.call-done = f32[256,128]{1,0:T(8,128)} async-done(((f32[256,1024]{1,0:T(8,128)}), f32[256,128]{1,0:T(8,128)}) %reduce-scatter.11.cloned.1.call-update) | async-done | bytes 131088 | tf_op jit(solution)/shard_map/reduce_scatter | solution.py:259
  444.0 67.1 %reduce-scatter.9.cloned.1.call-done = f32[128,256]{1,0:T(8,128)} async-done(((f32[1024,256]{1,0:T(8,128)}), f32[128,256]{1,0:T(8,128)}) %reduce-scatter.9.cloned.1.call-update) | async-done | bytes 131088 | tf_op jit(solution)/shard_map/reduce_scatter | solution.py:258
  511.1 71.6 %all-reduce.11.cloned.1.call-done = f32[1024,16]{0,1:T(8,128)} async-done(((f32[1024,16]{0,1:T(8,128)}), f32[1024,16]{0,1:T(8,128)}) %all-reduce.11.cloned.1.call-update) | async-done | bytes 65552 | tf_op jit(solution)/shard_map/psum | solution.py:264
  582.8 76.9 %reduce-scatter.13.cloned.1.call-done = f32[128,704]{0,1:T(8,128)} async-done(((f32[1024,704]{0,1:T(8,128)}), f32[128,704]{0,1:T(8,128)}) %reduce-scatter.13.cloned.1.call-update) | async-done | bytes 360464 | tf_op jit(solution)/shard_map/reduce_scatter | solution.py:178
  659.6 76.1 %reduce-scatter.15.cloned.1.call-done = f32[128,704]{0,1:T(8,128)} async-done(((f32[1024,704]{0,1:T(8,128)}), f32[128,704]{0,1:T(8,128)}) %reduce-scatter.15.cloned.1.call-update) | async-done | bytes 360464 | tf_op jit(solution)/shard_map/reduce_scatter | solution.py:179
  735.7 76.2 %reduce-scatter.17.cloned.1.call-done = f32[704,128]{1,0:T(8,128)} async-done(((f32[704,1024]{1,0:T(8,128)}), f32[704,128]{1,0:T(8,128)}) %reduce-scatter.17.cloned.1.call-update) | async-done | bytes 360464 | tf_op jit(solution)/shard_map/reduce_scatter | solution.py:180
  (343 shorter events, 109.7 us)
Async XLA Ops:
  7.2 113.6 %copy-start = (bf16[704,1024]{1,0:T(8,128)(2,1)S(1)}, bf16[704,1024]{1,0:T(8,128)(2,1)}, u32[]{:S(2)}) copy-start(bf16[704,1024]{1,0:T(8,128)(2,1)} %param.37) | copy-start | bytes 4325380
  7.2 60.4 %all-gather.7.cloned.1.call-start = ((), (), s32[]{:S(2)}) async-start(), calls=%async_computation.15 | async-start | bytes 1179648 | tf_op jit(solution)/shard_map/all_gather | solution.py:20
  11.1 6.3 collective-permute-start
  18.7 49.0 %copy-start.12 = (f32[1,256,128]{2,1,0:T(8,128)}, f32[1,256,128]{2,1,0:T(8,128)S(1)}, u32[]{:S(2)}) copy-start(f32[1,256,128]{2,1,0:T(8,128)S(1)} %slice.81) | copy-start | bytes 393220
  18.7 29.7 %copy-start.19 = (bf16[1,256,256]{2,1,0:T(8,128)(2,1)}, bf16[1,256,256]{2,1,0:T(8,128)(2,1)S(1)}, u32[]{:S(2)}) copy-start(bf16[1,256,256]{2,1,0:T(8,128)(2,1)S(1)} %slice.82) | copy-start | bytes 393220
  19.0 148.3 %copy-start.24 = (f32[1,4,64,128]{3,2,1,0:T(8,128)}, f32[1,4,64,128]{3,2,1,0:T(8,128)S(1)}, u32[]{:S(2)}) copy-start(f32[1,4,64,128]{3,2,1,0:T(8,128)S(1)} %get-tuple-element.560) | copy-start | bytes 393220
  24.6 50.9 %copy-start.16 = (f32[4,1,128,256]{3,2,1,0:T(8,128)}, f32[4,1,128,256]{3,2,1,0:T(8,128)S(1)}, u32[]{:S(2)}) copy-start(f32[4,1,128,256]{3,2,1,0:T(8,128)S(1)} %get-tuple-element.335) | copy-start | bytes 1572868
  25.3 90.6 %all-reduce.7.cloned.1.call-start = ((), (), s32[]{:S(2)}) async-start(), calls=%async_computation.6 | async-start | bytes 2097152 | tf_op jit(solution)/shard_map/psum | solution.py:161
  25.3 42.3 %copy-start.47 = (f32[64,64]{1,0:T(8,128)}, f32[64,64]{1,0:T(8,128)S(1)}, u32[]{:S(2)}) copy-start(f32[64,64]{1,0:T(8,128)S(1)} %fusion.102) | copy-start | bytes 49156
  48.4 28.7 %copy-start.34 = (f32[4,64,64]{2,1,0:T(8,128)}, f32[4,64,64]{2,1,0:T(8,128)S(1)}, u32[]{:S(2)}) copy-start(f32[4,64,64]{2,1,0:T(8,128)S(1)} %convolution_multiply_fusion.1) | copy-start | bytes 196612
  80.7 37.2 %copy-start.54 = (f32[1024]{0:T(1024)S(1)}, f32[1024]{0:T(1024)}, u32[]{:S(2)}) copy-start(f32[1024]{0:T(1024)} %param.34) | copy-start | bytes 12292
  80.7 81.4 %all-reduce.9.cloned.1.call-start = ((), (), s32[]{:S(2)}) async-start(), calls=%async_computation.7 | async-start | bytes 2097152 | tf_op jit(solution)/shard_map/psum | solution.py:182
  125.2 95.8 %all-gather.9.cloned.1.call-start = ((), (), s32[]{:S(2)}) async-start(), calls=%async_computation.16 | async-start | bytes 1179648 | tf_op jit(solution)/shard_map/all_gather | solution.py:20
  180.1 124.3 %all-reduce.13.cloned.1.call-start = ((), (), s32[]{:S(2)}) async-start(), calls=%async_computation.17 | async-start | bytes 4325376 | tf_op jit(solution)/shard_map/psum | solution.py:168
  244.5 5.7 collective-permute-start.1
  253.1 123.3 %reduce-scatter.7.cloned.1.call-start = ((), (), s32[]{:S(2)}) async-start(), calls=%async_computation.8 | async-start | bytes 2359296 | tf_op jit(solution)/shard_map/reduce_scatter | solution.py:257
  255.0 189.0 %reduce-scatter.11.cloned.1.call-start = ((), (), s32[]{:S(2)}) async-start(), calls=%async_computation.11 | async-start | bytes 1179648 | tf_op jit(solution)/shard_map/reduce_scatter | solution.py:259
  258.4 46.0 %copy-start.6 = (bf16[256,1024]{1,0:T(8,128)(2,1)S(1)}, bf16[256,1024]{1,0:T(8,128)(2,1)}, u32[]{:S(2)}) copy-start(bf16[256,1024]{1,0:T(8,128)(2,1)} %copy-done.5) | copy-start | bytes 1572868
  258.5 252.7 %reduce-scatter.9.cloned.1.call-start = ((), (), s32[]{:S(2)}) async-start(), calls=%async_computation.10 | async-start | bytes 1179648 | tf_op jit(solution)/shard_map/reduce_scatter | solution.py:258
  260.9 321.8 %all-reduce.11.cloned.1.call-start = ((), (), s32[]{:S(2)}) async-start(), calls=%async_computation.9 | async-start | bytes 131072 | tf_op jit(solution)/shard_map/psum | solution.py:264
  304.4 355.2 %reduce-scatter.13.cloned.1.call-start = ((), (), s32[]{:S(2)}) async-start(), calls=%async_computation.12 | async-start | bytes 3244032 | tf_op jit(solution)/shard_map/reduce_scatter | solution.py:178
  307.6 428.2 %reduce-scatter.15.cloned.1.call-start = ((), (), s32[]{:S(2)}) async-start(), calls=%async_computation.13 | async-start | bytes 3244032 | tf_op jit(solution)/shard_map/reduce_scatter | solution.py:179
  310.8 501.1 %reduce-scatter.17.cloned.1.call-start = ((), (), s32[]{:S(2)}) async-start(), calls=%async_computation.14 | async-start | bytes 3244032 | tf_op jit(solution)/shard_map/reduce_scatter | solution.py:180
  315.1 46.1 %copy-start.85 = (f32[256]{0:T(256)S(1)}, f32[256]{0:T(256)}, u32[]{:S(2)}) copy-start(f32[256]{0:T(256)} %get-tuple-element.552) | copy-start | bytes 3076
  (83 other events, 322.5 us)
Sparse Core Ops, SparseCore 0:
  25.4 42.2 all-gather.6
  80.8 34.9 all-reduce.6
  125.3 36.7 all-reduce.8
  180.2 40.7 all-gather.8
  253.2 51.1 all-reduce.12
  307.8 68.5 reduce-scatter.6
  380.3 63.6 reduce-scatter.10
  448.0 63.0 reduce-scatter.8
  514.5 68.1 all-reduce.10
  586.7 72.8 reduce-scatter.12
  663.8 71.9 reduce-scatter.14
  739.7 72.1 reduce-scatter.16
